TPU v7x, 32 devices: a whole 2x2x4 slice. The times are simulated.
32 devices in a mesh: replica: 8 (over y, x, core), shard: 4 (over z).
Axes of the slice: x: 2, y: 2, z: 4, core: 2. Of those that a mesh axis runs over, the one named last changes fastest.
Arguments:
- inputs: bfloat16 [4096, 2048], P(('replica', 'shard')), may hold values from -6 to 6
- lengths: int32 [8, 8], P('replica'), may hold values from 1 to 256, 512 in all within a row
- ln_gain: float32 [2048], replicated, may hold values from 0.5 to 1.5
- ln_bias: float32 [2048], replicated, may hold values from -3 to 3
- qkv_weight: bfloat16 [2048, 3, 2048], P(None, None, 'shard'), may hold values from -0.125 to 0.125
- qkv_bias: float32 [3, 2048], P(None, 'shard'), may hold values from -3 to 3
- out_weight: bfloat16 [2048, 2048], P('shard'), may hold values from -0.5 to 0.5
- fc1_weight: bfloat16 [2048, 8192], P(None, 'shard'), may hold values from -0.125 to 0.125
- fc1_bias: float32 [8192], P('shard'), may hold values from -3 to 3
- fc2_weight: bfloat16 [8192, 2048], P('shard'), may hold values from -0.0625 to 0.0625
- out_bias: float32 [2048], replicated, may hold values from -3 to 3
- cotangent: bfloat16 [4096, 2048], P(('replica', 'shard')), may hold values from -6 to 6
Outputs:
- output: bfloat16 [4096, 2048], P(('replica', 'shard'))
- input_grad: float32 [4096, 2048], P(('replica', 'shard'))
- ln_gain_grad: float32 [2048], P('shard')
- ln_bias_grad: float32 [2048], P('shard')
- qkv_weight_grad: float32 [2048, 3, 2048], P(None, None, 'shard')
- qkv_bias_grad: float32 [3, 2048], P(None, 'shard')
- out_weight_grad: float32 [2048, 2048], P('shard')
- fc1_weight_grad: float32 [2048, 8192], P(None, 'shard')
- fc1_bias_grad: float32 [8192], P('shard')
- fc2_weight_grad: float32 [8192, 2048], P('shard')
- out_bias_grad: float32 [2048], replicated
Inputs may be any that keep to these rules, and one draw needn't show every extreme that they name: Row g of lengths holds the lengths of the 8 sequences of replica group g in order; they add up to 512, and the longest is 256.
All inputs are finite; a program needn't handle non-finite values.
Results may differ from a plain program's by a relative error of at most 0.011.
Values may be sent and summed in bfloat16 or wider, within the bound.
No kernel may reach another device: no remote copies, remote signals or barrier semaphores. Data moves between devices by JAX's collectives and lax.ppermute only.
A program may use at most 320 MiB of HBM per device.

v0:
```python
import math
import jax
import jax.numpy as jnp
from jax import lax
from jax.sharding import PartitionSpec as P

HD = 64
ROT = 32


def normalize(x_float):
    mean_row = jnp.mean(x_float, axis=-1, keepdims=True)
    centred = x_float - mean_row
    inv_std = lax.rsqrt(jnp.mean(centred * centred, axis=-1, keepdims=True) + 1e-05)
    return (centred * inv_std, inv_std)


def positions(length_row, count):
    ends = jnp.cumsum(length_row, dtype=jnp.int32)
    row_ids = jnp.arange(count, dtype=jnp.int32)
    passed = (row_ids[:, None] >= ends[None, :]).astype(jnp.int32)
    segment = jnp.sum(passed, axis=1, dtype=jnp.int32)
    begin = jnp.sum(passed * length_row[None, :], axis=1, dtype=jnp.int32)
    offset = (row_ids - begin).astype(jnp.float32)
    freq_ids = jnp.arange(ROT // 2, dtype=jnp.float32)
    inverse = jnp.exp(freq_ids * (-2.0 * math.log(10000.0) / ROT))
    angle_rows = offset[:, None] * inverse[None, :]
    return (segment, row_ids, jnp.cos(angle_rows), jnp.sin(angle_rows))


def rotate(values, cosine, sine):
    half = ROT // 2
    first = values[..., :half]
    second = values[..., half:ROT]
    cos_b = cosine[:, None, :]
    sin_b = sine[:, None, :]
    return jnp.concatenate(
        [first * cos_b - second * sin_b, second * cos_b + first * sin_b, values[..., ROT:]], axis=-1
    )


def unrotate(values, cosine, sine):
    half = ROT // 2
    first = values[..., :half]
    second = values[..., half:ROT]
    cos_b = cosine[:, None, :]
    sin_b = sine[:, None, :]
    return jnp.concatenate(
        [first * cos_b + second * sin_b, second * cos_b - first * sin_b, values[..., ROT:]], axis=-1
    )


def gelu_tanh(inner):
    coef = math.sqrt(2.0 / math.pi)
    return 0.5 * inner * (1.0 + jnp.tanh(coef * (inner + 0.044715 * inner * inner * inner)))


def gelu_slope(inner):
    coef = math.sqrt(2.0 / math.pi)
    tangent = jnp.tanh(coef * (inner + 0.044715 * inner * inner * inner))
    return 0.5 * (1.0 + tangent) + 0.5 * inner * (1.0 - tangent * tangent) * coef * (
        1.0 + 3.0 * 0.044715 * inner * inner
    )


def allowed_mask(seg_block, row_block, segment, row_ids):
    return (seg_block[:, None] == segment[None, :]) & (row_ids[None, :] <= row_block[:, None])


def attend(query, keys, values, segment, row_ids):
    count, heads = (query.shape[0], query.shape[1])
    block = min(512, count)
    blocks = count // block

    def per_block(entry):
        q_block, seg_block, row_block = entry
        scores = (
            jnp.einsum("qhd,khd->hqk", q_block, keys, preferred_element_type=jnp.float32) * 0.125
        )
        allowed = allowed_mask(seg_block, row_block, segment, row_ids)[None]
        log_total = jnp.log(jnp.sum(jnp.where(allowed, jnp.exp(scores), 0.0), axis=-1))
        probs = jnp.where(allowed, jnp.exp(scores - log_total[..., None]), 0.0).astype(jnp.bfloat16)
        context = jnp.einsum(
            "hqk,khd->qhd", probs, values, preferred_element_type=jnp.float32
        ).astype(jnp.bfloat16)
        return (context, log_total)

    contexts, totals = lax.map(
        per_block,
        (
            query.reshape(blocks, block, heads, HD),
            segment.reshape(blocks, block),
            row_ids.reshape(blocks, block),
        ),
    )
    return (contexts.reshape(count, heads, HD), totals)


def attend_back(query, keys, values, totals, grad_context, segment, row_ids):
    count, heads = (query.shape[0], query.shape[1])
    block = min(512, count)
    blocks = count // block

    def per_block(carry, entry):
        grad_keys, grad_values = carry
        q_block, g_block, total_block, seg_block, row_block = entry
        scores = (
            jnp.einsum("qhd,khd->hqk", q_block, keys, preferred_element_type=jnp.float32) * 0.125
        )
        allowed = allowed_mask(seg_block, row_block, segment, row_ids)[None]
        probs = jnp.where(allowed, jnp.exp(scores - total_block[..., None]), 0.0)
        probs_low = probs.astype(jnp.bfloat16)
        grad_probs = jnp.einsum("qhd,khd->hqk", g_block, values, preferred_element_type=jnp.float32)
        grad_scores = (
            probs * (grad_probs - jnp.sum(probs * grad_probs, axis=-1, keepdims=True)) * 0.125
        ).astype(jnp.bfloat16)
        grad_query = jnp.einsum(
            "hqk,khd->qhd", grad_scores, keys, preferred_element_type=jnp.float32
        )
        grad_keys = grad_keys + jnp.einsum(
            "hqk,qhd->khd", grad_scores, q_block, preferred_element_type=jnp.float32
        )
        grad_values = grad_values + jnp.einsum(
            "hqk,qhd->khd", probs_low, g_block, preferred_element_type=jnp.float32
        )
        return ((grad_keys, grad_values), grad_query)

    zeros = jnp.zeros(keys.shape, jnp.float32)
    stacked = (
        query.reshape(blocks, block, heads, HD),
        grad_context.reshape(blocks, block, heads, HD),
        totals,
        segment.reshape(blocks, block),
        row_ids.reshape(blocks, block),
    )
    (grad_keys, grad_values), grad_queries = lax.scan(per_block, (zeros, zeros), stacked)
    return (grad_queries.reshape(count, heads, HD), grad_keys, grad_values)


def shards(
    inputs,
    lengths,
    ln_gain,
    ln_bias,
    qkv_weight,
    qkv_bias,
    out_weight,
    fc1_weight,
    fc1_bias,
    fc2_weight,
    out_bias,
    cotangent,
):
    rows_dev, width = inputs.shape
    qkv_flat = qkv_weight.reshape(width, -1)
    qkv_cols = qkv_flat.shape[1]
    heads_local = qkv_cols // (3 * HD)
    x_float = inputs.astype(jnp.float32)
    x_hat, inv_std = normalize(x_float)
    normed = (x_hat * ln_gain + ln_bias).astype(jnp.bfloat16)
    normed_full = lax.all_gather(normed, "shard", axis=0, tiled=True)
    qkv_pre = jnp.dot(normed_full, qkv_flat, preferred_element_type=jnp.float32)
    pre = jnp.dot(normed_full, fc1_weight, preferred_element_type=jnp.float32)
    group_rows = qkv_pre.shape[0]
    qkv = (qkv_pre + qkv_bias.reshape(-1)).reshape(group_rows, 3, heads_local, HD)
    segment, row_ids, cosine, sine = positions(lengths[0], group_rows)
    query = rotate(qkv[:, 0], cosine, sine).astype(jnp.bfloat16)
    keys = rotate(qkv[:, 1], cosine, sine).astype(jnp.bfloat16)
    values = qkv[:, 2].astype(jnp.bfloat16)
    context, totals = attend(query, keys, values, segment, row_ids)
    context_flat = context.reshape(group_rows, -1)
    pre = pre + fc1_bias
    hidden = gelu_tanh(pre).astype(jnp.bfloat16)
    mixed = lax.psum_scatter(
        jnp.dot(context_flat, out_weight, preferred_element_type=jnp.float32)
        + jnp.dot(hidden, fc2_weight, preferred_element_type=jnp.float32),
        "shard",
        scatter_dimension=0,
        tiled=True,
    )
    output = (x_float + mixed + out_bias).astype(jnp.bfloat16)
    cot_full = lax.all_gather(cotangent, "shard", axis=0, tiled=True)
    grad_out_w = jnp.dot(context_flat.T, cot_full, preferred_element_type=jnp.float32)
    grad_fc2 = jnp.dot(hidden.T, cot_full, preferred_element_type=jnp.float32)
    grad_out_b = jnp.sum(cot_full, axis=0, dtype=jnp.float32)
    grad_pre = jnp.dot(cot_full, fc2_weight.T, preferred_element_type=jnp.float32) * gelu_slope(pre)
    grad_fc1_b = jnp.sum(grad_pre, axis=0)
    grad_pre_low = grad_pre.astype(jnp.bfloat16)
    grad_fc1 = jnp.dot(normed_full.T, grad_pre_low, preferred_element_type=jnp.float32)
    grad_context = (
        jnp.dot(cot_full, out_weight.T, preferred_element_type=jnp.float32)
        .astype(jnp.bfloat16)
        .reshape(group_rows, heads_local, HD)
    )
    grad_query, grad_keys, grad_values = attend_back(
        query, keys, values, totals, grad_context, segment, row_ids
    )
    grad_qkv = jnp.stack(
        [unrotate(grad_query, cosine, sine), unrotate(grad_keys, cosine, sine), grad_values], axis=1
    ).reshape(group_rows, qkv_cols)
    grad_qkv_b = jnp.sum(grad_qkv, axis=0).reshape(qkv_bias.shape)
    grad_qkv_low = grad_qkv.astype(jnp.bfloat16)
    grad_qkv_w = jnp.dot(normed_full.T, grad_qkv_low, preferred_element_type=jnp.float32).reshape(
        qkv_weight.shape
    )
    grad_normed = lax.psum_scatter(
        jnp.dot(grad_qkv_low, qkv_flat.T, preferred_element_type=jnp.float32)
        + jnp.dot(grad_pre_low, fc1_weight.T, preferred_element_type=jnp.float32),
        "shard",
        scatter_dimension=0,
        tiled=True,
    )
    norm_parts = jnp.stack(
        [jnp.sum(grad_normed * x_hat, axis=0), jnp.sum(grad_normed, axis=0)], axis=0
    )
    norm_shares = lax.psum_scatter(norm_parts, "shard", scatter_dimension=1, tiled=True)
    scaled = grad_normed * ln_gain
    input_grad = cotangent.astype(jnp.float32) + inv_std * (
        scaled
        - jnp.mean(scaled, axis=-1, keepdims=True)
        - x_hat * jnp.mean(scaled * x_hat, axis=-1, keepdims=True)
    )
    grad_qkv_b, grad_fc1_b, grad_out_b, norm_shares = lax.psum(
        (grad_qkv_b, grad_fc1_b, grad_out_b, norm_shares), "replica"
    )
    low_sums = lax.psum(
        tuple((g.astype(jnp.bfloat16) for g in (grad_qkv_w, grad_out_w, grad_fc1, grad_fc2))),
        "replica",
    )
    grad_qkv_w, grad_out_w, grad_fc1, grad_fc2 = (g.astype(jnp.float32) for g in low_sums)
    return (
        output,
        input_grad,
        norm_shares[0],
        norm_shares[1],
        grad_qkv_w,
        grad_qkv_b,
        grad_out_w,
        grad_fc1,
        grad_fc1_b,
        grad_fc2,
        grad_out_b,
    )


def solution(mesh):
    placed = (
        P(("replica", "shard"), None),
        P("replica", None),
        P(),
        P(),
        P(None, None, "shard"),
        P(None, "shard"),
        P("shard", None),
        P(None, "shard"),
        P("shard"),
        P("shard", None),
        P(),
        P(("replica", "shard"), None),
    )
    return jax.shard_map(
        shards,
        mesh=mesh,
        in_specs=placed,
        out_specs=(
            P(("replica", "shard"), None),
            P(("replica", "shard"), None),
            P("shard"),
            P("shard"),
            P(None, None, "shard"),
            P(None, "shard"),
            P("shard", None),
            P(None, "shard"),
            P("shard"),
            P("shard", None),
            P(),
        ),
        check_vma=False,
    )
```

profile of v0, /device:TPU:0, one launch (start us, length us, event | category | flops | bytes accessed | tf_op | source)
XLA Modules:
  0.0 733.0 jit_solution(2110832071851290796)
XLA Ops:
  7.2 1.3 convert_reduce_fusion.1
  8.6 1.3 fusion.59
  9.9 2.3 fusion.53
  12.2 0.0 all-gather.5.cloned.1.call-start
  12.3 0.7 all-gather.5.cloned.1.call-update
  13.0 0.7 add.117
  13.7 8.8 %copy.45 = bf16[2048,3,512]{0,2,1:T(8,128)(2,1)} copy(bf16[2048,3,512]{2,0,1:T(8,128)(2,1)} %param.16) | data formatting | bytes 12582912 | tf_op args[4]
  22.5 0.2 reduce-window.8
  22.7 0.1 select_reduce_fusion.1
  22.8 0.2 multiply_cosine_fusion
  23.0 0.2 fusion.64
  23.2 37.5 %all-gather.3.cloned.1.call-done = bf16[512,2048]{1,0:T(8,128)(2,1)} async-done(((bf16[128,2048]{1,0:T(8,128)(2,1)}), bf16[512,2048]{1,0:T(8,128)(2,1)}) %all-gather.3.cloned.1.call-update) | async-done | bytes 2097168 | tf_op jit(solution)/shard_map/all_gather | solution.py:161
  60.7 8.5 %convolution_add_fusion.1 = f32[512,1536]{1,0:T(8,128)} fusion(bf16[512,2048]{1,0:T(8,128)(2,1)} %all-gather.3.cloned.1.call-done, bf16[2048,1536]{0,1:T(8,128)(2,1)} %bitcast.69, f32[1536]{0:T(1024)S(1)} %add.117), kind=kOutput, calls=%fused_computation.31 | convolution fusion | flops 3222011904 | bytes 11540480 | tf_op jit(solution)/shard_map/dot_general | solution.py:162
  69.3 3.6 copy.46
  72.9 1.8 slice_bitcast_fusion.1
  74.7 0.8 slice.114
  75.5 0.2 copy-done.6
  75.8 0.7 slice.113
  76.5 30.3 %all-gather.5.cloned.1.call-done = bf16[512,2048]{1,0:T(8,128)(2,1)} async-done(((bf16[128,2048]{1,0:T(8,128)(2,1)}), bf16[512,2048]{1,0:T(8,128)(2,1)}) %all-gather.5.cloned.1.call-update) | async-done | bytes 2097168 | tf_op jit(solution)/shard_map/all_gather | solution.py:182
  106.8 2.9 convolution_convert_fusion.4
  109.7 6.1 fusion.68
  115.8 1.0 subtract_convert_fusion.1
  116.8 9.1 %fusion.3 = f32[8,512,512]{1,2,0:T(8,128)} fusion(pred[512,512]{0,1:T(8,128)(4,1)S(1)} %fusion.64, bf16[512,8,32]{0,2,1:T(8,128)(2,1)} %slice.113, bf16[512,8,16]{0,2,1:T(8,128)(2,1)} %get-tuple-element.108, bf16[512,8,16]{0,2,1:T(8,128)(2,1)} %get-tuple-element.109, bf16[512,8,32]{0,2,1:T(8,128)(2,1)} %slice.114, ...), kind=kOutput, calls=%fused_computation.4 | convolution fusion | flops 553652736 | bytes 9699328 | tf_op jit(solution)/shard_map/while/body/eval_jaxpr/reduce_sum | solution.py:81
  125.9 5.0 fusion.34
  130.9 14.6 %fusion.37 = f32[512,8,64]{0,2,1:T(8,128)} fusion(f32[8,512,512]{1,2,0:T(8,128)} %fusion.3, f32[8,512,512]{1,2,0:T(8,128)} %fusion.68, bf16[512,8,32]{0,2,1:T(8,128)(2,1)} %slice.113, bf16[512,8,16]{0,2,1:T(8,128)(2,1)} %get-tuple-element.108, bf16[512,8,16]{0,2,1:T(8,128)(2,1)} %get-tuple-element.109), kind=kOutput, calls=%fused_computation.46 | convolution fusion | flops 280498688 | bytes 18350080 | tf_op jit(solution)/shard_map/while/body/eval_jaxpr/hqk,khd->qhd/dot_general | solution.py:117
  145.5 13.9 %fusion.40 = f32[512,8,64]{0,2,1:T(8,128)} fusion(f32[8,512,512]{1,2,0:T(8,128)} %fusion.3, f32[8,512,512]{1,2,0:T(8,128)} %fusion.68, bf16[512,8,32]{0,2,1:T(8,128)(2,1)S(1)} %copy-done.13, bf16[512,8,16]{0,2,1:T(8,128)(2,1)} %get-tuple-element.101, bf16[512,8,16]{0,2,1:T(8,128)(2,1)} %get-tuple-element.100), kind=kOutput, calls=%fused_computation.47 | convolution fusion | flops 280498688 | bytes 18350080 | tf_op jit(solution)/shard_map/while/body/eval_jaxpr/hqk,qhd->khd/dot_general | solution.py:120
  159.4 1.5 multiply_add_fusion.2
  160.9 0.2 maximum_bitcast_fusion
  161.2 0.4 fusion.28
  161.6 0.6 copy-done.3
  162.1 0.3 copy-done.4
  162.5 1.7 slice-done.1
  164.2 4.9 fusion.81
  169.2 6.1 fusion.80
  175.2 12.5 %fusion.79 = (f32[2048]{0:T(1024)S(1)}, bf16[512,2048]{1,0:T(8,128)(2,1)}) fusion(f32[512,2048]{1,0:T(8,128)} %fusion.80, f32[2048]{0:T(1024)S(1)} %copy-done.19, bf16[512,2048]{1,0:T(8,128)(2,1)S(1)} %copy-done.10, bf16[2048,2048]{1,0:T(8,128)(2,1)} %param.21), kind=kOutput, calls=%fused_computation.111 | convolution fusion | flops 4316985344 | bytes 16793600 | tf_op jit(solution)/shard_map/dot_general | solution.py:186
  187.8 7.7 %convolution_add_fusion.2 = f32[512,2048]{1,0:T(8,128)} fusion(f32[512,2048]{1,0:T(8,128)S(1)} %copy-done.20, bf16[2048,2048]{1,0:T(8,128)(2,1)S(1)} %bitcast.89, bf16[512,2048]{1,0:T(8,128)(2,1)} %get-tuple-element.115), kind=kOutput, calls=%fused_computation.33 | convolution fusion | flops 4296015872 | bytes 18874368 | tf_op jit(solution)/shard_map/dot_general | solution.py:208
  195.5 0.0 reduce-scatter.6.cloned.1.call-start
  195.6 4.7 fusion.43
  200.3 0.3 copy-done.21
  200.5 8.0 %fusion.77 = f32[512,2048]{1,0:T(8,128)S(1)} fusion(bf16[2048,2048]{1,0:T(8,128)(2,1)} %param.21, f32[512,2048]{1,0:T(8,128)S(1)} %copy-done.21, f32[2048]{0:T(1024)S(1)} %copy-done.19), kind=kOutput, calls=%fused_computation.109 | convolution fusion | flops 4305453056 | bytes 16785408 | tf_op jit(solution)/shard_map/dot_general | solution.py:176
  208.5 3.4 convolution_add_fusion
  211.9 0.3 reduce-scatter.10.cloned.1.call-start
  212.2 8.4 %convolution_convert_fusion.2 = bf16[2048,3,512]{2,0,1:T(8,128)(2,1)} fusion(bf16[3,512,512]{2,1,0:T(8,128)(2,1)} %bitcast.79, bf16[512,2048]{1,0:T(8,128)(2,1)} %all-gather.3.cloned.1.call-done), kind=kOutput, calls=%fused_computation.16 | convolution fusion | flops 3224371200 | bytes 9961472 | tf_op jit(solution)/shard_map/dot_general | solution.py:203
  220.6 6.8 convolution_convert_fusion.1
  227.5 7.6 %convolution_convert_fusion = bf16[2048,2048]{1,0:T(8,128)(2,1)} fusion(bf16[512,2048]{1,0:T(8,128)(2,1)S(1)} %copy-done.11, f32[512,2048]{1,0:T(8,128)S(1)} %copy-done.22, f32[2048]{0:T(1024)S(1)} %copy-done.19), kind=kOutput, calls=%fused_computation.11 | convolution fusion | flops 4309647360 | bytes 14688256 | tf_op jit(solution)/shard_map/dot_general | solution.py:184
  235.1 36.2 %reduce-scatter.8.cloned.1.call-done = f32[128,2048]{1,0:T(8,128)} async-done(((f32[512,2048]{1,0:T(8,128)}), f32[128,2048]{1,0:T(8,128)}) %reduce-scatter.8.cloned.1.call-update) | async-done | bytes 1048592 | tf_op jit(solution)/shard_map/reduce_scatter | solution.py:206
  271.3 1.7 fusion.58
  273.0 1.3 copy.58
  274.3 0.0 all-reduce.4.cloned.1.call-start
  274.4 4.2 convolution_convert_fusion.3
  278.6 2.9 fusion.27
  281.5 0.1 reshape.220
  281.6 2.0 convert_reduce_fusion
  283.5 67.2 %reduce-scatter.6.cloned.1.call-done = f32[128,2048]{1,0:T(8,128)} async-done(((f32[512,2048]{1,0:T(8,128)}), f32[128,2048]{1,0:T(8,128)}) %reduce-scatter.6.cloned.1.call-update) | async-done | bytes 1048592 | tf_op jit(solution)/shard_map/reduce_scatter | solution.py:174
  350.8 3.2 fusion.57
  354.0 26.7 %reduce-scatter.10.cloned.1.call-done = f32[512,2]{1,0:T(8,128)} async-done(((f32[2048,2]{1,0:T(8,128)}), f32[512,2]{1,0:T(8,128)}) %reduce-scatter.10.cloned.1.call-update) | async-done | bytes 4112
  380.7 1.1 copy.59
  381.8 26.0 %all-reduce = (f32[2,512]{1,0:T(2,128)S(1)}, f32[3,512]{1,0:T(4,128)}, f32[2048]{0:T(1024)}, f32[2048]{0:T(1024)}) all-reduce(f32[2,512]{1,0:T(2,128)S(1)} %copy.59, f32[3,512]{1,0:T(4,128)S(1)} %reshape.220, f32[2048]{0:T(1024)S(1)} %get-tuple-element.114, ...), channel_id=1, replica_groups=mesh['replica'=8,'shard'=4] {'replica'}, use_global_device_ids=true, to_apply=%region_14.15 | all-reduce | flops 6656 | bytes 53248 | tf_op jit(solution)/shard_map/psum | solution.py:223
  407.7 0.6 fusion.78
  408.3 283.3 %all-reduce.4.cloned.1.call-done = (bf16[2048,3,512]{2,0,1:T(8,128)(2,1)}, bf16[512,2048]{1,0:T(8,128)(2,1)}, bf16[2048,2048]{1,0:T(8,128)(2,1)}, bf16[2048,2048]{1,0:T(8,128)(2,1)}) async-done(((bf16[2048,3,512]{2,0,1:T(8,128)(2,1)}, bf16[512,2048]{1,0:T(8,128)(2,1)}, bf16[2048,2048]{1,0:T(8,128)(2,1)}, bf16[2048,2048]{1,0:T(8,128)(2,1)}), (bf16[2048,3,512]{2,0,1:T(8,128)(2,1)}, ...) | async-done | bytes 25165840 | tf_op jit(solution)/shard_map/psum | solution.py:226
  691.7 4.3 convert_element_type.113
  695.9 6.6 convert_element_type.111
  702.5 11.7 %convert_element_type.115 = f32[2048,2048]{1,0:T(8,128)} convert(bf16[2048,2048]{1,0:T(8,128)(2,1)} %get-tuple-element.92) | non-fusion elementwise | flops 4194304 | bytes 25165824 | tf_op jit(solution)/shard_map/convert_element_type | solution.py:230
  714.2 11.7 %convert_element_type.117 = f32[2048,2048]{1,0:T(8,128)} convert(bf16[2048,2048]{1,0:T(8,128)(2,1)} %get-tuple-element.93) | non-fusion elementwise | flops 4194304 | bytes 25165824 | tf_op jit(solution)/shard_map/convert_element_type | solution.py:230
  (71 shorter events, 0.4 us)
Async XLA Ops:
  7.2 99.6 %copy-start = (bf16[512,2048]{1,0:T(8,128)(2,1)S(1)}, bf16[512,2048]{1,0:T(8,128)(2,1)}, u32[]{:S(2)}) copy-start(bf16[512,2048]{1,0:T(8,128)(2,1)} %param.18) | copy-start | bytes 6291460
  7.2 53.5 %all-gather.3.cloned.1.call-start = ((), (), s32[]{:S(2)}) async-start(), calls=%async_computation.3 | async-start | bytes 2621440 | tf_op jit(solution)/shard_map/all_gather | solution.py:161
  12.2 94.6 %all-gather.5.cloned.1.call-start = ((), (), s32[]{:S(2)}) async-start(), calls=%async_computation.5 | async-start | bytes 2621440 | tf_op jit(solution)/shard_map/all_gather | solution.py:182
  13.0 258.3 %reduce-scatter.8.cloned.1.call-start = ((), (), s32[]{:S(2)}) async-start(), calls=%async_computation.6 | async-start | bytes 5242880 | tf_op jit(solution)/shard_map/reduce_scatter | solution.py:206
  13.7 8.8 %copy-start.16 = (s32[1,8]{1,0:T(1,128)S(1)}, s32[1,8]{1,0:T(1,128)}, u32[]{:S(2)}) copy-start(s32[1,8]{1,0:T(1,128)} %param.13) | copy-start | bytes 100
  74.7 1.1 copy-start.6
  109.7 6.1 copy-start.8
  109.7 6.1 copy-start.7
  130.8 30.3 %copy-start.2 = (f32[512,1,8,64]{0,3,2,1:T(8,128)}, f32[512,1,8,64]{0,3,2,1:T(8,128)S(1)}, u32[]{:S(2)}) copy-start(f32[512,1,8,64]{0,3,2,1:T(8,128)S(1)} %fusion.34) | copy-start | bytes 3145732
  130.9 14.6 %copy-start.13 = (bf16[512,8,32]{0,2,1:T(8,128)(2,1)S(1)}, bf16[512,8,32]{0,2,1:T(8,128)(2,1)}, u32[]{:S(2)}) copy-start(bf16[512,8,32]{0,2,1:T(8,128)(2,1)} %slice.114) | copy-start | bytes 786436
  159.4 1.5 slice-start.2
  159.4 1.5 slice-start.3
  159.4 3.1 slice-start
  160.9 3.3 slice-start.1
  161.2 1.0 copy-start.3
  161.2 1.3 copy-start.4
  161.2 7.9 %slice-start.4 = ((s8[8388608]{0:T(1024)(128)(4,1)}), s8[4194304]{0:T(1024)(128)(4,1)S(1)}, s32[]{:S(2)}) async-start(s8[8388608]{0:T(1024)(128)(4,1)} %bitcast.88), calls=%async_computation.13 | async-start | bytes 8388608
  162.5 6.6 copy-start.12
  164.2 5.0 slice-start.5
  164.2 5.0 copy-start.17
  169.1 6.1 copy-start.10
  169.1 6.1 copy-start.19
  175.2 12.6 %copy-start.20 = (f32[512,2048]{1,0:T(8,128)S(1)}, f32[512,2048]{1,0:T(8,128)}, u32[]{:S(2)}) copy-start(f32[512,2048]{1,0:T(8,128)} %fusion.81) | copy-start | bytes 12582916
  195.5 155.2 %reduce-scatter.6.cloned.1.call-start = ((), (), s32[]{:S(2)}) async-start(), calls=%async_computation.4 | async-start | bytes 5242880 | tf_op jit(solution)/shard_map/reduce_scatter | solution.py:174
  195.6 5.0 copy-start.21
  211.9 168.8 %reduce-scatter.10.cloned.1.call-start = ((), (), s32[]{:S(2)}) async-start(), calls=%async_computation.7 | async-start | bytes 1310720
  212.2 8.4 %copy-start.18 = (bf16[512,2048]{1,0:T(8,128)(2,1)S(1)}, bf16[512,2048]{1,0:T(8,128)(2,1)}, u32[]{:S(2)}) copy-start(bf16[512,2048]{1,0:T(8,128)(2,1)} %all-gather.3.cloned.1.call-done) | copy-start | bytes 6291460
  212.2 8.4 %copy-start.23 = (bf16[512,2048]{1,0:T(8,128)(2,1)S(1)}, bf16[512,2048]{1,0:T(8,128)(2,1)}, u32[]{:S(2)}) copy-start(bf16[512,2048]{1,0:T(8,128)(2,1)} %get-tuple-element.115) | copy-start | bytes 6291460
  220.6 6.9 copy-start.11
  220.6 6.9 copy-start.22
  227.5 43.8 %copy-start.1 = (bf16[128,2048]{1,0:T(8,128)(2,1)S(1)}, bf16[128,2048]{1,0:T(8,128)(2,1)}, u32[]{:S(2)}) copy-start(bf16[128,2048]{1,0:T(8,128)(2,1)} %param.12) | copy-start | bytes 1572868
  227.5 43.8 %copy-start.14 = (f32[2048]{0:T(1024)S(1)}, f32[2048]{0:T(1024)}, u32[]{:S(2)}) copy-start(f32[2048]{0:T(1024)} %param.14) | copy-start | bytes 24580
  274.3 417.3 %all-reduce.4.cloned.1.call-start = ((), (), s32[]{:S(2)}) async-start(), calls=%async_computation.8 | async-start | bytes 50331648 | tf_op jit(solution)/shard_map/psum | solution.py:226
  278.6 72.2 %copy-start.9 = (bf16[128,2048]{1,0:T(8,128)(2,1)S(1)}, bf16[128,2048]{1,0:T(8,128)(2,1)}, u32[]{:S(2)}) copy-start(bf16[128,2048]{1,0:T(8,128)(2,1)} %param.23) | copy-start | bytes 1572868
  278.6 72.1 %copy-start.15 = (f32[2048]{0:T(1024)S(1)}, f32[2048]{0:T(1024)}, u32[]{:S(2)}) copy-start(f32[2048]{0:T(1024)} %param.22) | copy-start | bytes 24580
  691.7 4.3 copy-start.5
Sparse Core Ops, SparseCore 0:
  12.3 48.3 all-gather.2
  62.3 44.4 all-gather.4
  195.6 75.5 reduce-scatter.7
  273.4 77.2 reduce-scatter.5
  352.9 27.7 reduce-scatter.9
  385.9 305.6 all-reduce.3
where the time goes:
time: 741 us; the launch traced here: 733 us
  waiting for transfers between devices  482 us (65%)
  matrix products  134 us (18%)
  other arithmetic  52.6 us (7%)
  blocking collectives  26 us (4%)
  local copies, waits for them, and re-layouts  22.7 us (3%)
  between operations  14.7 us (2%)
    psum x1, waiting for transfers between devices, shards(): lax.psum(tuple((g.astype(jnp.bfloat16) for g in (grad_qkv_w, grad_out_w,...  283 us
    reduce_scatter x1, waiting for transfers between devices, shards(): lax.psum_scatter(jnp.dot(context_flat, out_weight, preferred_element_type...  67.2 us
    all_gather x1, waiting for transfers between devices, shards(): normed_full = lax.all_gather(normed, 'shard', axis=0, tiled=True)  37.5 us
    reduce_scatter x1, waiting for transfers between devices, shards(): lax.psum_scatter(jnp.dot(grad_qkv_low, qkv_flat.T, preferred_element_type...  36.2 us
    convert_element_type x4, other arithmetic, shards(): g.astype(jnp.float32)  34.2 us
    all_gather x1, waiting for transfers between devices, shards(): cot_full = lax.all_gather(cotangent, 'shard', axis=0, tiled=True)  30.3 us
    unnamed x7, waiting for transfers between devices  27.5 us
    psum x1, blocking collectives, shards(): lax.psum((grad_qkv_b, grad_fc1_b, grad_out_b, norm_shares), 'replica')  26 us
  transfers between devices with their start and end apart: 6, of which 6 were waited for; matrix products, arithmetic and copies ran while one was open for 11% of the time, Pallas kernels for 0%

commit v1 on v0

--- a/solution.py
+++ b/solution.py
@@ -158,7 +158,14 @@
     x_float = inputs.astype(jnp.float32)
     x_hat, inv_std = normalize(x_float)
     normed = (x_hat * ln_gain + ln_bias).astype(jnp.bfloat16)
-    normed_full = lax.all_gather(normed, "shard", axis=0, tiled=True)
+    ring = [normed]
+    for hop in range(3):
+        ring.append(lax.ppermute(ring[-1], "shard", [(dev, (dev + 1) % 4) for dev in range(4)]))
+    normed_full = jnp.roll(
+        jnp.concatenate(ring[::-1], axis=0),
+        (lax.axis_index("shard") + 1) * ring[0].shape[0],
+        axis=0,
+    )
     qkv_pre = jnp.dot(normed_full, qkv_flat, preferred_element_type=jnp.float32)
     pre = jnp.dot(normed_full, fc1_weight, preferred_element_type=jnp.float32)
     group_rows = qkv_pre.shape[0]

time: 741 us -> 729 us (0.984)
  waiting for transfers between devices: 482 us -> 469 us
    ppermute x0 -> x3, waiting for transfers between devices: none -> 46.4 us  [shards(): lax.ppermute(ring[-1], 'shard', [(dev, (dev + 1) % 4) for dev in range(4)])]
    all_gather x1 -> x0, waiting for transfers between devices: 37.5 us -> none  [shards(): normed_full = lax.all_gather(normed, 'shard', axis=0, tiled=True)]
    all_gather x1, waiting for transfers between devices: 30.3 us -> 0.01 us  [shards(): cot_full = lax.all_gather(cotangent, 'shard', axis=0, tiled=True)]
    reduce_scatter x1, waiting for transfers between devices: 36.2 us -> 44.8 us  [shards(): lax.psum_scatter(jnp.dot(grad_qkv_low, qkv_flat.T, preferred_element_type...]
    unnamed x59 -> x69, local copies, waits for them, and re-layouts: 14.4 us -> 20.3 us
    unnamed x7 -> x6, waiting for transfers between devices: 27.5 us -> 26.8 us
  transfers between devices with their start and end apart: 6 -> 8, of which waited for: 6 -> 7; matrix products, arithmetic and copies ran while one was open for 11% -> 14% of each run, Pallas kernels for 0% -> 0%
where the time goes in v1:
time: 729 us; the launch traced here: 723 us
  waiting for transfers between devices  469 us (64%)
  matrix products  130 us (18%)
  other arithmetic  53.2 us (7%)
  local copies, waits for them, and re-layouts  27.6 us (4%)
  blocking collectives  26 us (4%)
  between operations  14.5 us (2%)
    psum x1, waiting for transfers between devices, shards(): lax.psum(tuple((g.astype(jnp.bfloat16) for g in (grad_qkv_w, grad_out_w,...  283 us
    reduce_scatter x1, waiting for transfers between devices, shards(): lax.psum_scatter(jnp.dot(context_flat, out_weight, preferred_element_type...  67.5 us
    ppermute x3, waiting for transfers between devices, shards(): lax.ppermute(ring[-1], 'shard', [(dev, (dev + 1) % 4) for dev in range(4)])  46.4 us
    reduce_scatter x1, waiting for transfers between devices, shards(): lax.psum_scatter(jnp.dot(grad_qkv_low, qkv_flat.T, preferred_element_type...  44.8 us
    convert_element_type x4, other arithmetic, shards(): g.astype(jnp.float32)  34.2 us
    unnamed x6, waiting for transfers between devices  26.8 us
    psum x1, blocking collectives, shards(): lax.psum((grad_qkv_b, grad_fc1_b, grad_out_b, norm_shares), 'replica')  26 us
    unnamed x69, local copies, waits for them, and re-layouts  20.3 us
  transfers between devices with their start and end apart: 8, of which 7 were waited for; matrix products, arithmetic and copies ran while one was open for 14% of the time, Pallas kernels for 0%

profile of v1, /device:TPU:0, one launch (start us, length us, event | category | flops | bytes accessed | tf_op | source)
XLA Modules:
  0.0 723.2 jit_solution(7400975058335595648)
XLA Ops:
  7.2 1.3 convert_reduce_fusion.1
  8.6 1.3 fusion.64
  9.9 1.5 fusion.58
  11.4 3.1 collective-permute-start
  14.5 13.9 %collective-permute-done = bf16[128,2048]{1,0:T(8,128)(2,1)S(1)} collective-permute-done((bf16[128,2048]{1,0:T(8,128)(2,1)S(1)}, bf16[128,2048]{1,0:T(8,128)(2,1)S(1)}, u32[]{:S(2)}, u32[]{:S(2)}) %collective-permute-start) | collective-permute-done | bytes 524320 | tf_op jit(solution)/shard_map/ppermute | solution.py:163
  28.5 0.8 reduce-window.8
  29.4 0.7 add.133
  30.1 8.9 %copy.45 = bf16[2048,3,512]{0,2,1:T(8,128)(2,1)} copy(bf16[2048,3,512]{2,0,1:T(8,128)(2,1)} %param.16) | data formatting | bytes 12582912 | tf_op args[4]
  39.0 0.1 select_reduce_fusion.1
  39.1 6.3 collective-permute-done.1
  45.4 0.2 multiply_cosine_fusion
  45.6 0.2 fusion.69
  45.9 26.1 %collective-permute-done.2 = bf16[128,2048]{1,0:T(8,128)(2,1)S(1)} collective-permute-done((bf16[128,2048]{1,0:T(8,128)(2,1)}, bf16[128,2048]{1,0:T(8,128)(2,1)S(1)}, u32[]{:S(2)}, u32[]{:S(2)}) %collective-permute-start.2) | collective-permute-done | bytes 524320 | tf_op jit(solution)/shard_map/ppermute | solution.py:163
  72.1 1.1 constant_dynamic-update-slice_fusion.6
  73.2 0.4 constant_dynamic-update-slice_fusion.4
  73.7 1.1 constant_dynamic-update-slice_fusion.2
  74.8 0.4 constant_dynamic-update-slice_fusion
  75.2 1.9 copy-done.15
  77.2 5.1 convolution_add_fusion.1
  82.3 4.1 copy.46
  86.4 1.8 slice_bitcast_fusion.1
  88.3 0.9 subtract_convert_fusion.1
  89.2 8.2 %fusion.3 = f32[8,512,512]{1,2,0:T(8,128)} fusion(pred[512,512]{0,1:T(8,128)(4,1)S(1)} %fusion.69, bf16[512,8,32]{0,2,1:T(8,128)(2,1)S(1)} %slice.113, bf16[512,8,16]{0,2,1:T(8,128)(2,1)} %get-tuple-element.108, bf16[512,8,16]{0,2,1:T(8,128)(2,1)} %get-tuple-element.109, bf16[512,8,32]{0,2,1:T(8,128)(2,1)S(1)} %slice.114, ...), kind=kOutput, calls=%fused_computation.4 | convolution fusion | flops 553652736 | bytes 9699328 | tf_op jit(solution)/shard_map/while/body/eval_jaxpr/reduce_sum | solution.py:81
  97.4 10.5 %fusion.45 = f32[512,2048]{1,0:T(8,128)} fusion(bf16[2048,2048]{1,0:T(8,128)(2,1)} %param.19, bf16[1024,2048]{1,0:T(8,128)(2,1)} %copy-done.15, s32[]{:T(128)S(6)} %select_n.25), kind=kOutput, calls=%fused_computation.50 | convolution fusion | flops 4294967296 | bytes 14680068 | tf_op jit(solution)/shard_map/dot_general | solution.py:170
  107.9 3.0 convolution_convert_fusion.4
  110.9 6.1 fusion.73
  117.0 2.4 fusion.34
  119.4 14.2 %fusion.37 = f32[512,8,64]{0,2,1:T(8,128)} fusion(f32[8,512,512]{1,2,0:T(8,128)} %fusion.3, f32[8,512,512]{1,2,0:T(8,128)} %fusion.73, bf16[512,8,32]{0,2,1:T(8,128)(2,1)S(1)} %slice.113, bf16[512,8,16]{0,2,1:T(8,128)(2,1)} %get-tuple-element.108, bf16[512,8,16]{0,2,1:T(8,128)(2,1)} %get-tuple-element.109), kind=kOutput, calls=%fused_computation.46 | convolution fusion | flops 280498688 | bytes 18350080 | tf_op jit(solution)/shard_map/while/body/eval_jaxpr/hqk,khd->qhd/dot_general | solution.py:117
  133.6 13.0 %fusion.40 = f32[512,8,64]{0,2,1:T(8,128)} fusion(f32[8,512,512]{1,2,0:T(8,128)} %fusion.3, f32[8,512,512]{1,2,0:T(8,128)} %fusion.73, bf16[512,8,32]{0,2,1:T(8,128)(2,1)S(1)} %slice.114, bf16[512,8,16]{0,2,1:T(8,128)(2,1)S(1)} %copy-done.13, bf16[512,8,16]{0,2,1:T(8,128)(2,1)S(1)} %copy-done.12), kind=kOutput, calls=%fused_computation.47 | convolution fusion | flops 280498688 | bytes 18350080 | tf_op jit(solution)/shard_map/while/body/eval_jaxpr/hqk,qhd->khd/dot_general | solution.py:120
  146.6 1.5 multiply_add_fusion.2
  148.1 0.2 maximum_bitcast_fusion
  148.4 0.4 fusion.28
  148.8 0.6 copy-done.3
  149.3 0.3 copy-done.4
  149.6 0.9 slice-done.2
  150.6 1.3 slice-done.3
  151.9 5.1 fusion.89
  157.0 11.4 %fusion.88 = (f32[2048]{0:T(1024)S(1)}, bf16[512,2048]{1,0:T(8,128)(2,1)S(1)}) fusion(f32[512,2048]{1,0:T(8,128)} %fusion.45, f32[2048]{0:T(1024)S(1)} %copy-done.19, bf16[512,2048]{1,0:T(8,128)(2,1)S(1)} %copy-done.8, bf16[2048,2048]{1,0:T(8,128)(2,1)} %param.21), kind=kOutput, calls=%fused_computation.128 | convolution fusion | flops 4316985344 | bytes 16793600 | tf_op jit(solution)/shard_map/dot_general | solution.py:193
  168.4 1.3 copy-done.22
  169.7 7.7 %convolution_add_fusion.2 = f32[512,2048]{1,0:T(8,128)} fusion(f32[512,2048]{1,0:T(8,128)} %fusion.89, bf16[2048,2048]{1,0:T(8,128)(2,1)S(1)} %bitcast.88, bf16[512,2048]{1,0:T(8,128)(2,1)S(1)} %get-tuple-element.115), kind=kOutput, calls=%fused_computation.33 | convolution fusion | flops 4296015872 | bytes 18874368 | tf_op jit(solution)/shard_map/dot_general | solution.py:215
  177.5 4.7 fusion.48
  182.2 0.2 copy-done.20
  182.4 7.9 %fusion.86 = f32[512,2048]{1,0:T(8,128)S(1)} fusion(bf16[2048,2048]{1,0:T(8,128)(2,1)} %param.21, f32[512,2048]{1,0:T(8,128)S(1)} %copy-done.20, f32[2048]{0:T(1024)S(1)} %copy-done.19), kind=kOutput, calls=%fused_computation.126 | convolution fusion | flops 4305453056 | bytes 16785408 | tf_op jit(solution)/shard_map/dot_general | solution.py:183
  190.3 3.4 convolution_add_fusion
  193.8 8.4 %convolution_convert_fusion.2 = bf16[2048,3,512]{2,0,1:T(8,128)(2,1)} fusion(bf16[3,512,512]{2,1,0:T(8,128)(2,1)} %bitcast.78, bf16[1024,2048]{1,0:T(8,128)(2,1)} %copy-done.15, s32[]{:T(128)S(6)} %select_n.25), kind=kOutput, calls=%fused_computation.16 | convolution fusion | flops 3224371200 | bytes 9961476 | tf_op jit(solution)/shard_map/dot_general | solution.py:210
  202.3 7.1 convolution_convert_fusion.1
  209.4 7.5 %convolution_convert_fusion = bf16[2048,2048]{1,0:T(8,128)(2,1)} fusion(bf16[512,2048]{1,0:T(8,128)(2,1)S(1)} %copy-done.9, f32[512,2048]{1,0:T(8,128)S(1)} %copy-done.21, f32[2048]{0:T(1024)S(1)} %copy-done.19), kind=kOutput, calls=%fused_computation.11 | convolution fusion | flops 4309647360 | bytes 14688256 | tf_op jit(solution)/shard_map/dot_general | solution.py:191
  216.9 44.8 %reduce-scatter.8.cloned.1.call-done = f32[128,2048]{1,0:T(8,128)} async-done(((f32[512,2048]{1,0:T(8,128)}), f32[128,2048]{1,0:T(8,128)}) %reduce-scatter.8.cloned.1.call-update) | async-done | bytes 1048592 | tf_op jit(solution)/shard_map/reduce_scatter | solution.py:213
  261.7 1.7 fusion.63
  263.4 1.4 copy.58
  264.8 4.2 convolution_convert_fusion.3
  269.0 2.7 fusion.27
  271.9 2.0 convert_reduce_fusion
  273.9 67.5 %reduce-scatter.6.cloned.1.call-done = f32[128,2048]{1,0:T(8,128)} async-done(((f32[512,2048]{1,0:T(8,128)}), f32[128,2048]{1,0:T(8,128)}) %reduce-scatter.6.cloned.1.call-update) | async-done | bytes 1048592 | tf_op jit(solution)/shard_map/reduce_scatter | solution.py:181
  341.3 3.3 fusion.62
  344.6 26.7 %reduce-scatter.10.cloned.1.call-done = f32[512,2]{1,0:T(8,128)} async-done(((f32[2048,2]{1,0:T(8,128)}), f32[512,2]{1,0:T(8,128)}) %reduce-scatter.10.cloned.1.call-update) | async-done | bytes 4112
  371.3 1.1 copy.59
  372.3 26.0 %all-reduce = (f32[2,512]{1,0:T(2,128)S(1)}, f32[3,512]{1,0:T(4,128)}, f32[2048]{0:T(1024)}, f32[2048]{0:T(1024)}) all-reduce(f32[2,512]{1,0:T(2,128)S(1)} %copy.59, f32[3,512]{1,0:T(4,128)S(1)} %reshape.220, f32[2048]{0:T(1024)S(1)} %get-tuple-element.114, ...), channel_id=1, replica_groups=mesh['replica'=8,'shard'=4] {'replica'}, use_global_device_ids=true, to_apply=%region_14.15 | all-reduce | flops 6656 | bytes 53248 | tf_op jit(solution)/shard_map/psum | solution.py:230
  398.4 0.6 fusion.87
  398.9 283.3 %all-reduce.4.cloned.1.call-done = (bf16[2048,3,512]{2,0,1:T(8,128)(2,1)}, bf16[512,2048]{1,0:T(8,128)(2,1)}, bf16[2048,2048]{1,0:T(8,128)(2,1)}, bf16[2048,2048]{1,0:T(8,128)(2,1)}) async-done(((bf16[2048,3,512]{2,0,1:T(8,128)(2,1)}, bf16[512,2048]{1,0:T(8,128)(2,1)}, bf16[2048,2048]{1,0:T(8,128)(2,1)}, bf16[2048,2048]{1,0:T(8,128)(2,1)}), (bf16[2048,3,512]{2,0,1:T(8,128)(2,1)}, ...) | async-done | bytes 25165840 | tf_op jit(solution)/shard_map/psum | solution.py:233
  682.2 4.3 convert_element_type.113
  686.5 6.6 convert_element_type.111
  693.1 11.7 %convert_element_type.115 = f32[2048,2048]{1,0:T(8,128)} convert(bf16[2048,2048]{1,0:T(8,128)(2,1)} %get-tuple-element.92) | non-fusion elementwise | flops 4194304 | bytes 25165824 | tf_op jit(solution)/shard_map/convert_element_type | solution.py:237
  704.7 11.7 %convert_element_type.117 = f32[2048,2048]{1,0:T(8,128)} convert(bf16[2048,2048]{1,0:T(8,128)(2,1)} %get-tuple-element.93) | non-fusion elementwise | flops 4194304 | bytes 25165824 | tf_op jit(solution)/shard_map/convert_element_type | solution.py:237
  (87 shorter events, 0.8 us)
Async XLA Ops:
  7.2 100.7 %copy-start = (bf16[512,2048]{1,0:T(8,128)(2,1)S(1)}, bf16[512,2048]{1,0:T(8,128)(2,1)}, u32[]{:S(2)}) copy-start(bf16[512,2048]{1,0:T(8,128)(2,1)} %param.18) | copy-start | bytes 6291460
  7.2 100.7 %all-gather.2.cloned.1.call-start = ((), (), s32[]{:S(2)}) async-start(), calls=%async_computation.4 | async-start | bytes 2621440 | tf_op jit(solution)/shard_map/all_gather | solution.py:189
  11.4 17.1 %collective-permute-start = (bf16[128,2048]{1,0:T(8,128)(2,1)S(1)}, bf16[128,2048]{1,0:T(8,128)(2,1)S(1)}, u32[]{:S(2)}, u32[]{:S(2)}) collective-permute-start(bf16[128,2048]{1,0:T(8,128)(2,1)S(1)} %fusion.58), channel_id=1, source_target_pairs={{0,1},{1,2},{2,3},{3,0},{4,5},{5,6},{6,7},{7,4},{8,9},{9,10},{10,1... | collective-permute-start | bytes 1572872 | tf_op jit(solution)/shard_map/ppermute | solution.py:163
  28.4 17.0 %collective-permute-start.1 = (bf16[128,2048]{1,0:T(8,128)(2,1)S(1)}, bf16[128,2048]{1,0:T(8,128)(2,1)}, u32[]{:S(2)}, u32[]{:S(2)}) collective-permute-start(bf16[128,2048]{1,0:T(8,128)(2,1)S(1)} %collective-permute-done), channel_id=1, source_target_pairs={{0,1},{1,2},{2,3},{3,0},{4,5},{5,6},{6,7},{7,4},{8,9},{9,10},{10,1... | collective-permute-start | bytes 1572872 | tf_op jit(solution)/shard_map/ppermute | solution.py:163
  28.5 233.2 %reduce-scatter.8.cloned.1.call-start = ((), (), s32[]{:S(2)}) async-start(), calls=%async_computation.5 | async-start | bytes 5242880 | tf_op jit(solution)/shard_map/reduce_scatter | solution.py:213
  30.1 8.9 %copy-start.18 = (s32[1,8]{1,0:T(1,128)S(1)}, s32[1,8]{1,0:T(1,128)}, u32[]{:S(2)}) copy-start(s32[1,8]{1,0:T(1,128)} %param.13) | copy-start | bytes 100
  30.1 43.1 %copy-start.1 = (bf16[128,2048]{1,0:T(8,128)(2,1)S(1)}, bf16[128,2048]{1,0:T(8,128)(2,1)}, u32[]{:S(2)}) copy-start(bf16[128,2048]{1,0:T(8,128)(2,1)} %param.12) | copy-start | bytes 1572868
  30.1 43.1 %copy-start.11 = (f32[2048]{0:T(1024)S(1)}, f32[2048]{0:T(1024)}, u32[]{:S(2)}) copy-start(f32[2048]{0:T(1024)} %param.14) | copy-start | bytes 24580
  30.1 43.1 %copy-start.14 = (f32[2048]{0:T(1024)S(1)}, f32[2048]{0:T(1024)}, u32[]{:S(2)}) copy-start(f32[2048]{0:T(1024)} %param.15) | copy-start | bytes 24580
  45.4 26.6 %collective-permute-start.2 = (bf16[128,2048]{1,0:T(8,128)(2,1)}, bf16[128,2048]{1,0:T(8,128)(2,1)S(1)}, u32[]{:S(2)}, u32[]{:S(2)}) collective-permute-start(bf16[128,2048]{1,0:T(8,128)(2,1)} %collective-permute-done.1), channel_id=1, source_target_pairs={{0,1},{1,2},{2,3},{3,0},{4,5},{5,6},{6,7},{7,4},{8,9},{9,10},{10,1... | collective-permute-start | bytes 1572872 | tf_op jit(solution)/shard_map/ppermute | solution.py:163
  45.9 31.3 %copy-start.5 = (bf16[2048,3,512]{0,2,1:T(8,128)(2,1)S(1)}, bf16[2048,3,512]{0,2,1:T(8,128)(2,1)}, u32[]{:S(2)}) copy-start(bf16[2048,3,512]{0,2,1:T(8,128)(2,1)} %copy.45) | copy-start | bytes 18874372
  75.2 2.0 copy-start.15
  107.9 9.1 %slice-start = ((s8[8388608]{0:T(1024)(128)(4,1)}), s8[4194304]{0:T(1024)(128)(4,1)S(1)}, s32[]{:S(2)}) async-start(s8[8388608]{0:T(1024)(128)(4,1)} %bitcast.63), calls=%async_computation.8 | async-start | bytes 8388608
  110.9 6.1 slice-start.1
  119.4 14.2 %copy-start.12 = (bf16[512,8,16]{0,2,1:T(8,128)(2,1)S(1)}, bf16[512,8,16]{0,2,1:T(8,128)(2,1)}, u32[]{:S(2)}) copy-start(bf16[512,8,16]{0,2,1:T(8,128)(2,1)} %get-tuple-element.100) | copy-start | bytes 393220
  119.4 14.2 %copy-start.13 = (bf16[512,8,16]{0,2,1:T(8,128)(2,1)S(1)}, bf16[512,8,16]{0,2,1:T(8,128)(2,1)}, u32[]{:S(2)}) copy-start(bf16[512,8,16]{0,2,1:T(8,128)(2,1)} %get-tuple-element.101) | copy-start | bytes 393220
  146.6 1.5 slice-start.4
  146.6 1.5 slice-start.5
  146.6 1.9 copy-start.2
  146.6 4.0 slice-start.2
  148.1 3.8 slice-start.3
  148.3 1.0 copy-start.3
  148.4 1.3 copy-start.4
  149.3 7.6 %copy-start.10 = (bf16[512,3,8,64]{0,3,2,1:T(8,128)(2,1)}, bf16[512,3,8,64]{0,3,2,1:T(8,128)(2,1)S(1)}, u32[]{:S(2)}) copy-start(bf16[512,3,8,64]{0,3,2,1:T(8,128)(2,1)S(1)} %fusion.28) | copy-start | bytes 4718596
  151.9 5.1 copy-start.8
  151.9 5.1 copy-start.19
  151.9 17.8 %slice-start.6 = ((s8[8388608]{0:T(1024)(128)(4,1)}), s8[4194304]{0:T(1024)(128)(4,1)S(1)}, s32[]{:S(2)}) async-start(s8[8388608]{0:T(1024)(128)(4,1)} %bitcast.87), calls=%async_computation.14 | async-start | bytes 8388608
  157.0 12.7 %slice-start.7 = ((s8[8388608]{0:T(1024)(128)(4,1)}), s8[4194304]{0:T(1024)(128)(4,1)S(1)}, s32[]{:S(2)}) async-start(s8[8388608]{0:T(1024)(128)(4,1)} %bitcast.87), calls=%async_computation.15 | async-start | bytes 8388608
  168.4 1.3 copy-start.22
  177.4 163.9 %reduce-scatter.6.cloned.1.call-start = ((), (), s32[]{:S(2)}) async-start(), calls=%async_computation.3 | async-start | bytes 5242880 | tf_op jit(solution)/shard_map/reduce_scatter | solution.py:181
  177.5 4.9 copy-start.20
  193.8 177.5 %reduce-scatter.10.cloned.1.call-start = ((), (), s32[]{:S(2)}) async-start(), calls=%async_computation.6 | async-start | bytes 1310720
  193.8 8.4 %copy-start.16 = (bf16[1024,2048]{1,0:T(8,128)(2,1)S(1)}, bf16[1024,2048]{1,0:T(8,128)(2,1)}, u32[]{:S(2)}) copy-start(bf16[1024,2048]{1,0:T(8,128)(2,1)} %copy-done.15) | copy-start | bytes 12582916
  193.8 8.4 %copy-start.23 = (bf16[512,2048]{1,0:T(8,128)(2,1)S(1)}, bf16[512,2048]{1,0:T(8,128)(2,1)}, u32[]{:S(2)}) copy-start(bf16[512,2048]{1,0:T(8,128)(2,1)} %copy-done.22) | copy-start | bytes 6291460
  202.2 7.1 copy-start.9
  202.2 7.1 copy-start.21
  264.8 417.4 %all-reduce.4.cloned.1.call-start = ((), (), s32[]{:S(2)}) async-start(), calls=%async_computation.7 | async-start | bytes 50331648 | tf_op jit(solution)/shard_map/psum | solution.py:233
  269.0 72.3 %copy-start.7 = (bf16[128,2048]{1,0:T(8,128)(2,1)S(1)}, bf16[128,2048]{1,0:T(8,128)(2,1)}, u32[]{:S(2)}) copy-start(bf16[128,2048]{1,0:T(8,128)(2,1)} %param.23) | copy-start | bytes 1572868
  269.0 72.3 %copy-start.17 = (f32[2048]{0:T(1024)S(1)}, f32[2048]{0:T(1024)}, u32[]{:S(2)}) copy-start(f32[2048]{0:T(1024)} %param.22) | copy-start | bytes 24580
  682.2 4.3 copy-start.6
Sparse Core Ops, SparseCore 0:
  28.6 60.2 all-gather.1
  177.6 84.0 reduce-scatter.7
  264.0 77.2 reduce-scatter.5
  343.5 27.7 reduce-scatter.9
  376.5 305.6 all-reduce.3
